TPU v7x, 32 devices: a whole 2x2x4 slice. The times are simulated.
32 devices in a mesh: group: 4 (over y, x), member: 8 (over z, core).
Axes of the slice: x: 2, y: 2, z: 4, core: 2. Of those that a mesh axis runs over, the one named last changes fastest.
Arguments:
- activations: bfloat16 [4, 1024, 2048], P('group', 'member'), may hold values from -6 to 6
- lengths: int32 [4, 8], P('group'), may hold values from 1 to 128, 576 in all within a row
- assignment: int32 [4, 8], P('group'), may hold values from 0 to 7, each once within a row
- owners: int32 [4], replicated, may hold values from 0 to 3
- prefix_cache: bfloat16 [4, 8192, 256], P('group', 'member'), may hold values from -244 to 244
- first_gain: float32 [2048], replicated, may hold values from 0.1 to 1.9
- first_bias: float32 [2048], replicated, may hold values from -3 to 3
- query_weight: bfloat16 [2048, 2048], replicated, may hold values from -0.125 to 0.125
- keyval_weight: bfloat16 [2048, 256], replicated, may hold values from -0.4375 to 0.4375
- output_weight: bfloat16 [2048, 2048], replicated, may hold values from -0.125 to 0.125
- second_gain: float32 [2048], replicated, may hold values from 0.1 to 1.9
- second_bias: float32 [2048], replicated, may hold values from -3 to 3
- expand_weight: bfloat16 [2048, 8192], P(None, 'member'), may hold values from -0.125 to 0.125
- contract_weight: bfloat16 [8192, 2048], P('member'), may hold values from -0.0625 to 0.0625
Outputs:
- layer_output: bfloat16 [4, 1024, 2048], P('group', 'member')
Inputs may be any that keep to these rules, and one draw needn't show every extreme that they name: Each row of lengths sums to 576 and its longest entry is 128. Each row of assignment names every request of its group once. `owners`: several groups may attend the same cache slot.
All inputs are finite; a program needn't handle non-finite values.
Results may differ from a plain program's by a relative error of at most 0.011.
The roundings to bfloat16 on the way count: a program that leaves them out, or rounds other values in their place, can miss the bound.
Values may be sent and summed in bfloat16 or wider, within the bound.
No kernel may reach another device: no remote copies, remote signals or barrier semaphores. Data moves between devices by JAX's collectives and lax.ppermute only.
A program may use at most 128 MiB of HBM per device.

v0:
```python
import math
import jax
import jax.numpy as jnp
from jax import lax
from jax.sharding import PartitionSpec as P

EPSILON = 1e-05
NEGATIVE = -1e30


def layer_norm(values, gain, bias):
    average = jnp.mean(values, axis=-1, keepdims=True)
    centered = values - average
    spread = jnp.mean(centered * centered, axis=-1, keepdims=True)
    return centered * lax.rsqrt(spread + EPSILON) * gain + bias


def pick_value(table, wanted):
    slots_at = lax.broadcasted_iota(jnp.int32, table.shape, 0)
    return jnp.sum(jnp.where(slots_at == wanted, table, 0))


def own_scores(query_block, own_keys, scaling):
    scores = (
        jnp.einsum("thd,sd->ths", query_block, own_keys, preferred_element_type=jnp.float32)
        * scaling
    )
    block_rows = query_block.shape[0]
    key_rows = own_keys.shape[0]
    row_at = lax.broadcasted_iota(jnp.int32, (block_rows, 1, key_rows), 0)
    column_at = lax.broadcasted_iota(jnp.int32, (block_rows, 1, key_rows), 2)
    return jnp.where(column_at <= row_at, scores, NEGATIVE)


def folded_attention(queries, keys_values, selected):
    row_count, head_count, head_size = queries.shape
    scaling = 1.0 / math.sqrt(head_size)
    own_keys = keys_values[:, :head_size]
    own_values = keys_values[:, head_size:]
    suffix_scores = own_scores(queries, own_keys, scaling)
    highest = jnp.max(suffix_scores, axis=-1)
    suffix_exp = jnp.exp(suffix_scores - highest[..., None])
    denominator = jnp.sum(suffix_exp, axis=-1)
    weighted = jnp.einsum(
        "ths,sd->thd",
        suffix_exp.astype(jnp.bfloat16),
        own_values,
        preferred_element_type=jnp.float32,
    )
    running = (weighted, highest, denominator)
    portion = lax.all_gather(selected, "member", axis=0, tiled=True)
    extent = portion.shape[0]
    stride = math.gcd(extent, 1024)

    def advance(state_now, block_index):
        weighted_now, highest_now, denominator_now = state_now
        key_block = lax.dynamic_slice_in_dim(portion, block_index * stride, stride, 0)
        scores = (
            jnp.einsum(
                "thd,pd->thp", queries, key_block[:, :head_size], preferred_element_type=jnp.float32
            )
            * scaling
        )
        highest_next = jnp.maximum(highest_now, jnp.max(scores, axis=-1))
        rescale = jnp.exp(highest_now - highest_next)
        exponent = jnp.exp(scores - highest_next[..., None])
        denominator_next = denominator_now * rescale + jnp.sum(exponent, axis=-1)
        weighted_next = weighted_now * rescale[..., None] + jnp.einsum(
            "thp,pd->thd",
            exponent.astype(jnp.bfloat16),
            key_block[:, head_size:],
            preferred_element_type=jnp.float32,
        )
        return ((weighted_next, highest_next, denominator_next), None)

    running, _ = lax.scan(advance, running, jnp.arange(extent // stride, dtype=jnp.int32))
    weighted, highest, denominator = running
    return (
        (weighted / denominator[..., None])
        .astype(jnp.bfloat16)
        .reshape(row_count, head_count * head_size)
    )


def shards(
    activations,
    lengths,
    assignment,
    owners,
    prefix_cache,
    first_gain,
    first_bias,
    query_weight,
    keyval_weight,
    output_weight,
    second_gain,
    second_bias,
    expand_weight,
    contract_weight,
):
    group_index = lax.axis_index("group")
    member_index = lax.axis_index("member")
    request = pick_value(assignment[0], member_index)
    length_here = pick_value(lengths[0], request)
    owner_here = pick_value(owners, group_index)
    tokens = activations[0]
    row_count = tokens.shape[0]
    head_size = prefix_cache.shape[2] // 2
    head_count = tokens.shape[1] // head_size
    every_block = lax.all_gather(prefix_cache, "group", axis=0, tiled=True)
    selected = lax.dynamic_index_in_dim(every_block, owner_here, 0, keepdims=False)
    tokens_wide = tokens.astype(jnp.float32)
    normed = layer_norm(tokens_wide, first_gain, first_bias).astype(jnp.bfloat16)
    queries = jnp.dot(normed, query_weight, preferred_element_type=jnp.float32).astype(jnp.bfloat16)
    queries = queries.reshape(row_count, head_count, head_size)
    keys_values = jnp.dot(normed, keyval_weight, preferred_element_type=jnp.float32).astype(
        jnp.bfloat16
    )
    attended = folded_attention(queries, keys_values, selected)
    residual = tokens_wide + jnp.dot(attended, output_weight, preferred_element_type=jnp.float32)
    second = layer_norm(residual, second_gain, second_bias).astype(jnp.bfloat16)
    hidden = jax.nn.gelu(
        jnp.dot(
            lax.all_gather(second, "member", axis=0, tiled=True),
            expand_weight,
            preferred_element_type=jnp.float32,
        ),
        approximate=True,
    ).astype(jnp.bfloat16)
    summed = lax.psum_scatter(
        jnp.dot(hidden, contract_weight, preferred_element_type=jnp.float32).astype(jnp.bfloat16),
        "member",
        scatter_dimension=0,
        tiled=True,
    ).astype(jnp.float32)
    is_live = lax.broadcasted_iota(jnp.int32, (row_count, 1), 0) < length_here
    return jnp.where(is_live, residual + summed, 0.0).astype(jnp.bfloat16)[None]


def solution(mesh):
    return jax.shard_map(
        shards,
        mesh=mesh,
        in_specs=(
            P("group", "member", None),
            P("group", None),
            P("group", None),
            P(),
            P("group", "member", None),
            P(),
            P(),
            P(),
            P(),
            P(),
            P(),
            P(),
            P(None, "member"),
            P("member", None),
        ),
        out_specs=P("group", "member", None),
        check_vma=False,
    )
```

profile of v0, /device:TPU:0, one launch (start us, length us, event | category | flops | bytes accessed | tf_op | source)
XLA Modules:
  0.0 286.6 jit_solution(2638500522030421383)
XLA Ops:
  10.5 36.7 %all-gather.5.cloned.1.call-done = bf16[4,1024,256]{2,1,0:T(8,128)(2,1)} async-done(((bf16[1,1024,256]{2,1,0:T(8,128)(2,1)}), bf16[4,1024,256]{2,1,0:T(8,128)(2,1)}) %all-gather.5.cloned.1.call-update) | async-done | bytes 2097168 | tf_op jit(solution)/shard_map/all_gather | solution.py:110
  47.2 1.9 constant_dynamic-slice_fusion
  51.8 5.0 %fusion.30 = bf16[16,16,8,128]{3,2,1,0:T(8,128)(2,1)S(1)} fusion(bf16[2048,2048]{1,0:T(8,128)(2,1)} %param.23, bf16[1,128,2048]{2,1,0:T(8,128)(2,1)} %param.16, f32[2048]{0:T(1024)} %param.22, f32[2048]{0:T(1024)} %param.21, f32[128]{0:T(128)S(1)} %add_rsqrt_fusion.1, f32[128]{0:T(128)S(1)} %broadcast_multiply_fusion.1), kind=kOutput, calls=%fused_computation.39 | convolution fusion | flops 1075576832 | bytes 9454592 | tf_op jit(solution)/shard_map/dot_general | solution.py:114
  58.2 38.3 %all-gather.9.cloned.1.call-done = bf16[1,8192,256]{2,1,0:T(8,128)(2,1)} async-done(((bf16[1,1024,256]{2,1,0:T(8,128)(2,1)}), bf16[1,8192,256]{2,1,0:T(8,128)(2,1)}) %all-gather.9.cloned.1.call-update) | async-done | bytes 4194320 | tf_op jit(solution)/shard_map/all_gather | solution.py:51
  96.4 62.7 %while.14 = (s32[]{:T(128)}, f32[128,16,128]{2,0,1:T(8,128)S(1)}, f32[128,16]{0,1:T(8,128)S(1)}, f32[128,16]{0,1:T(8,128)S(1)}, s32[8]{0:T(128)S(1)}, /*index=5*...) while((s32[]{:T(128)}, f32[128,16,128]{2,0,1:T(8,128)S(1)}, ...), condition=%wide.region_10.11_spmd, body=%wide.region_7.10_spmd.sunk | while | flops 1091047424 | bytes 28442832 | solution.py:76
  97.7 2.2 bitcast_reduce_fusion.2
  99.9 1.4 fusion.68
  101.3 2.9 %fusion.69 = f32[128,16,128]{2,0,1:T(8,128)S(1)} fusion(f32[1024,128,16]{1,0,2:T(8,128)S(1)} %get-tuple-element.135, f32[128,16]{0,1:T(8,128)S(1)} %max.4, f32[128,16,128]{2,0,1:T(8,128)S(1)} %get-tuple-element.152, f32[128,16]{0,1:T(8,128)S(1)} %get-tuple-element.137, bf16[8192,256]{1,0:T(8,128)(2,1)} %get-tuple-element.168, s32[]{:T(128)S(6)} %select_n.46, ...), kind=kOutput, calls=%fused_computation.8.clone.1 | convolution fusion | flops 543686656 | bytes 10764296 | tf_op jit(solution)/shard_map/while/body/eval_jaxpr/thp,pd->thd/dot_general | solution.py:68
  105.5 2.2 bitcast_reduce_fusion.2
  107.8 1.4 fusion.68
  109.2 2.9 %fusion.69 = f32[128,16,128]{2,0,1:T(8,128)S(1)} fusion(f32[1024,128,16]{1,0,2:T(8,128)S(1)} %get-tuple-element.135, f32[128,16]{0,1:T(8,128)S(1)} %max.4, f32[128,16,128]{2,0,1:T(8,128)S(1)} %get-tuple-element.152, f32[128,16]{0,1:T(8,128)S(1)} %get-tuple-element.137, bf16[8192,256]{1,0:T(8,128)(2,1)} %get-tuple-element.168, s32[]{:T(128)S(6)} %select_n.46, ...), kind=kOutput, calls=%fused_computation.8.clone.1 | convolution fusion | flops 543686656 | bytes 10764296 | tf_op jit(solution)/shard_map/while/body/eval_jaxpr/thp,pd->thd/dot_general | solution.py:68
  113.4 2.2 bitcast_reduce_fusion.2
  115.6 1.4 fusion.68
  117.0 2.9 %fusion.69 = f32[128,16,128]{2,0,1:T(8,128)S(1)} fusion(f32[1024,128,16]{1,0,2:T(8,128)S(1)} %get-tuple-element.135, f32[128,16]{0,1:T(8,128)S(1)} %max.4, f32[128,16,128]{2,0,1:T(8,128)S(1)} %get-tuple-element.152, f32[128,16]{0,1:T(8,128)S(1)} %get-tuple-element.137, bf16[8192,256]{1,0:T(8,128)(2,1)} %get-tuple-element.168, s32[]{:T(128)S(6)} %select_n.46, ...), kind=kOutput, calls=%fused_computation.8.clone.1 | convolution fusion | flops 543686656 | bytes 10764296 | tf_op jit(solution)/shard_map/while/body/eval_jaxpr/thp,pd->thd/dot_general | solution.py:68
  121.2 2.2 bitcast_reduce_fusion.2
  123.4 1.4 fusion.68
  124.8 2.9 %fusion.69 = f32[128,16,128]{2,0,1:T(8,128)S(1)} fusion(f32[1024,128,16]{1,0,2:T(8,128)S(1)} %get-tuple-element.135, f32[128,16]{0,1:T(8,128)S(1)} %max.4, f32[128,16,128]{2,0,1:T(8,128)S(1)} %get-tuple-element.152, f32[128,16]{0,1:T(8,128)S(1)} %get-tuple-element.137, bf16[8192,256]{1,0:T(8,128)(2,1)} %get-tuple-element.168, s32[]{:T(128)S(6)} %select_n.46, ...), kind=kOutput, calls=%fused_computation.8.clone.1 | convolution fusion | flops 543686656 | bytes 10764296 | tf_op jit(solution)/shard_map/while/body/eval_jaxpr/thp,pd->thd/dot_general | solution.py:68
  129.0 2.2 bitcast_reduce_fusion.2
  131.3 1.4 fusion.68
  132.7 2.9 %fusion.69 = f32[128,16,128]{2,0,1:T(8,128)S(1)} fusion(f32[1024,128,16]{1,0,2:T(8,128)S(1)} %get-tuple-element.135, f32[128,16]{0,1:T(8,128)S(1)} %max.4, f32[128,16,128]{2,0,1:T(8,128)S(1)} %get-tuple-element.152, f32[128,16]{0,1:T(8,128)S(1)} %get-tuple-element.137, bf16[8192,256]{1,0:T(8,128)(2,1)} %get-tuple-element.168, s32[]{:T(128)S(6)} %select_n.46, ...), kind=kOutput, calls=%fused_computation.8.clone.1 | convolution fusion | flops 543686656 | bytes 10764296 | tf_op jit(solution)/shard_map/while/body/eval_jaxpr/thp,pd->thd/dot_general | solution.py:68
  136.9 2.2 bitcast_reduce_fusion.2
  139.1 1.4 fusion.68
  140.5 2.9 %fusion.69 = f32[128,16,128]{2,0,1:T(8,128)S(1)} fusion(f32[1024,128,16]{1,0,2:T(8,128)S(1)} %get-tuple-element.135, f32[128,16]{0,1:T(8,128)S(1)} %max.4, f32[128,16,128]{2,0,1:T(8,128)S(1)} %get-tuple-element.152, f32[128,16]{0,1:T(8,128)S(1)} %get-tuple-element.137, bf16[8192,256]{1,0:T(8,128)(2,1)} %get-tuple-element.168, s32[]{:T(128)S(6)} %select_n.46, ...), kind=kOutput, calls=%fused_computation.8.clone.1 | convolution fusion | flops 543686656 | bytes 10764296 | tf_op jit(solution)/shard_map/while/body/eval_jaxpr/thp,pd->thd/dot_general | solution.py:68
  144.7 2.2 bitcast_reduce_fusion.2
  148.4 2.9 %fusion.69 = f32[128,16,128]{2,0,1:T(8,128)S(1)} fusion(f32[1024,128,16]{1,0,2:T(8,128)S(1)} %get-tuple-element.135, f32[128,16]{0,1:T(8,128)S(1)} %max.4, f32[128,16,128]{2,0,1:T(8,128)S(1)} %get-tuple-element.152, f32[128,16]{0,1:T(8,128)S(1)} %get-tuple-element.137, bf16[8192,256]{1,0:T(8,128)(2,1)} %get-tuple-element.168, s32[]{:T(128)S(6)} %select_n.46, ...), kind=kOutput, calls=%fused_computation.8.clone.1 | convolution fusion | flops 543686656 | bytes 10764296 | tf_op jit(solution)/shard_map/while/body/eval_jaxpr/thp,pd->thd/dot_general | solution.py:68
  152.6 2.2 bitcast_reduce_fusion.2
  156.2 2.9 %fusion.69 = f32[128,16,128]{2,0,1:T(8,128)S(1)} fusion(f32[1024,128,16]{1,0,2:T(8,128)S(1)} %get-tuple-element.135, f32[128,16]{0,1:T(8,128)S(1)} %max.4, f32[128,16,128]{2,0,1:T(8,128)S(1)} %get-tuple-element.152, f32[128,16]{0,1:T(8,128)S(1)} %get-tuple-element.137, bf16[8192,256]{1,0:T(8,128)(2,1)} %get-tuple-element.168, s32[]{:T(128)S(6)} %select_n.46, ...), kind=kOutput, calls=%fused_computation.8.clone.1 | convolution fusion | flops 543686656 | bytes 10764296 | tf_op jit(solution)/shard_map/while/body/eval_jaxpr/thp,pd->thd/dot_general | solution.py:68
  161.9 4.8 %fusion.51 = (f32[128]{0:T(128)S(1)}, f32[128,2048]{1,0:T(8,128)S(1)}) fusion(bf16[128,2048]{0,1:T(8,128)(2,1)S(1)} %bitcast.88, bf16[2048,2048]{1,0:T(8,128)(2,1)} %param.25, bf16[1,128,2048]{2,1,0:T(8,128)(2,1)S(1)} %copy-done.1), kind=kOutput, calls=%fused_computation.76 | convolution fusion | flops 1074528128 | bytes 10486272 | tf_op jit(solution)/shard_map/dot_general | solution.py:120
  168.2 45.8 %all-gather.7.cloned.1.call-done = bf16[1024,2048]{1,0:T(8,128)(2,1)} async-done(((bf16[128,2048]{1,0:T(8,128)(2,1)}), bf16[1024,2048]{1,0:T(8,128)(2,1)}) %all-gather.7.cloned.1.call-update) | async-done | bytes 4194320 | tf_op jit(solution)/shard_map/all_gather | solution.py:124
  214.0 15.1 %convolution_convert_fusion = bf16[1024,2048]{1,0:T(8,128)(2,1)} fusion(bf16[1024,2048]{1,0:T(8,128)(2,1)} %param.29, bf16[1024,2048]{1,0:T(8,128)(2,1)} %all-gather.7.cloned.1.call-done, bf16[2048,1024]{1,0:T(8,128)(2,1)} %param.28), kind=kOutput, calls=%fused_computation.25 | convolution fusion | flops 8601468928 | bytes 16777216 | tf_op jit(solution)/shard_map/dot_general | solution.py:131
  232.2 45.8 %reduce-scatter.2.cloned.1.call-done = bf16[128,2048]{1,0:T(8,128)(2,1)} async-done(((bf16[1024,2048]{1,0:T(8,128)(2,1)}), bf16[128,2048]{1,0:T(8,128)(2,1)}) %reduce-scatter.2.cloned.1.call-update) | async-done | bytes 524304 | tf_op jit(solution)/shard_map/reduce_scatter | solution.py:130
  278.0 2.0 fusion.39
  (79 shorter events, 20.9 us)
Async XLA Ops:
  6.5 50.4 %copy-start = (bf16[2048,256]{1,0:T(8,128)(2,1)S(1)}, bf16[2048,256]{1,0:T(8,128)(2,1)}, u32[]{:S(2)}) copy-start(bf16[2048,256]{1,0:T(8,128)(2,1)} %param.24) | copy-start | bytes 3145732
  6.5 40.7 %all-gather.5.cloned.1.call-start = ((), (), s32[]{:S(2)}) async-start(), calls=%async_computation.1 | async-start | bytes 2621440 | tf_op jit(solution)/shard_map/all_gather | solution.py:110
  7.3 89.2 %all-gather.9.cloned.1.call-start = ((), (), s32[]{:S(2)}) async-start(), calls=%async_computation.4 | async-start | bytes 4718592 | tf_op jit(solution)/shard_map/all_gather | solution.py:51
  49.1 164.9 %all-gather.7.cloned.1.call-start = ((), (), s32[]{:S(2)}) async-start(), calls=%async_computation.2 | async-start | bytes 4718592 | tf_op jit(solution)/shard_map/all_gather | solution.py:124
  51.7 5.2 %copy-start.1 = (bf16[1,128,2048]{2,1,0:T(8,128)(2,1)S(1)}, bf16[1,128,2048]{2,1,0:T(8,128)(2,1)}, u32[]{:S(2)}) copy-start(bf16[1,128,2048]{2,1,0:T(8,128)(2,1)} %param.16) | copy-start | bytes 1572868
  51.7 5.2 %copy-start.4 = (f32[2048]{0:T(1024)S(1)}, f32[2048]{0:T(1024)}, u32[]{:S(2)}) copy-start(f32[2048]{0:T(1024)} %param.22) | copy-start | bytes 24580
  51.8 5.2 %copy-start.5 = (f32[2048]{0:T(1024)S(1)}, f32[2048]{0:T(1024)}, u32[]{:S(2)}) copy-start(f32[2048]{0:T(1024)} %param.21) | copy-start | bytes 24580
  161.8 5.1 %copy-start.2 = (f32[2048]{0:T(1024)S(1)}, f32[2048]{0:T(1024)}, u32[]{:S(2)}) copy-start(f32[2048]{0:T(1024)} %param.27) | copy-start | bytes 24580
  161.9 5.1 %copy-start.3 = (f32[2048]{0:T(1024)S(1)}, f32[2048]{0:T(1024)}, u32[]{:S(2)}) copy-start(f32[2048]{0:T(1024)} %param.26) | copy-start | bytes 24580
  168.0 110.1 %reduce-scatter.2.cloned.1.call-start = ((), (), s32[]{:S(2)}) async-start(), calls=%async_computation.3 | async-start | bytes 4718592 | tf_op jit(solution)/shard_map/reduce_scatter | solution.py:130
  229.1 0.7 copy-start.6
  229.1 1.3 copy-start.7
Sparse Core Ops, SparseCore 0:
  9.2 38.0 all-gather.4
  49.3 47.1 all-gather.8
  168.1 45.8 all-gather.6
  229.3 48.7 reduce-scatter.1
where the time goes:
time: 288 us; the launch traced here: 287 us
  waiting for transfers between devices  167 us (58%)
  matrix products  67.1 us (23%)
  other arithmetic  22.2 us (8%)
  between operations  15.2 us (5%)
  local copies, waits for them, and re-layouts  8.7 us (3%)
  loops' own time  5.68 us (2%)
    reduce_scatter x1, waiting for transfers between devices, shards(): lax.psum_scatter(jnp.dot(hidden, contract_weight, preferred_element_type=...  45.8 us
    all_gather x1, waiting for transfers between devices, shards(): lax.all_gather(second, 'member', axis=0, tiled=True)  45.8 us
    all_gather x1, waiting for transfers between devices, folded_attention(): portion = lax.all_gather(selected, 'member', axis=0, tiled=True)  38.3 us
    all_gather x1, waiting for transfers between devices, shards(): every_block = lax.all_gather(prefix_cache, 'group', axis=0, tiled=True)  36.7 us
    dot_general x8, matrix products, advance(): jnp.einsum('thp,pd->thd', exponent.astype(jnp.bfloat16), key_block[:, hea...  23.5 us
    dot_general x8, matrix products, advance(): jnp.einsum('thd,pd->thp', queries, key_block[:, :head_size], preferred_el...  17.7 us
    dot_general x1, matrix products, shards(): jnp.dot(hidden, contract_weight, preferred_element_type=jnp.float32)  15.1 us
    reduce_sum x8, other arithmetic, advance(): denominator_next = denominator_now * rescale + jnp.sum(exponent, axis=-1)  11 us
  transfers between devices with their start and end apart: 4, of which 4 were waited for; matrix products, arithmetic and copies ran while one was open for 4% of the time, Pallas kernels for 0%

commit v1 on v0

--- a/solution.py
+++ b/solution.py
@@ -6,6 +6,16 @@
 
 EPSILON = 1e-05
 NEGATIVE = -1e30
+
+
+def gather_around(x, axis, dim):
+    ways, here, step = (lax.axis_size(axis), lax.axis_index(axis), x.shape[dim])
+    dims = [n * ways if d == dim else n for d, n in enumerate(x.shape)]
+    full = lax.dynamic_update_slice_in_dim(jnp.zeros(dims, x.dtype), x, here * step, axis=dim)
+    for far in range(1, ways):
+        x = lax.ppermute(x, axis, [(d, (d + 1) % ways) for d in range(ways)])
+        full = lax.dynamic_update_slice_in_dim(full, x, (here - far) % ways * step, axis=dim)
+    return full
 
 
 def layer_norm(values, gain, bias):
@@ -121,9 +131,7 @@
     second = layer_norm(residual, second_gain, second_bias).astype(jnp.bfloat16)
     hidden = jax.nn.gelu(
         jnp.dot(
-            lax.all_gather(second, "member", axis=0, tiled=True),
-            expand_weight,
-            preferred_element_type=jnp.float32,
+            gather_around(second, "member", 0), expand_weight, preferred_element_type=jnp.float32
         ),
         approximate=True,
     ).astype(jnp.bfloat16)

time: 288 us -> 344 us (1.19)
  local copies, waits for them, and re-layouts: 8.7 us -> 34.7 us
  waiting for transfers between devices: 167 us -> 185 us
  matrix products: 67.1 us -> 79.4 us
    ppermute x0 -> x7, waiting for transfers between devices: none -> 64.5 us  [gather_around(): x = lax.ppermute(x, axis, [(d, (d + 1) % ways) for d in range(ways)])]
    all_gather x1 -> x0, waiting for transfers between devices: 45.8 us -> none  [shards(): lax.all_gather(second, 'member', axis=0, tiled=True)]
    while x8 -> x24, local copies, waits for them, and re-layouts: 0.02 us -> 14.4 us
    dot_general x8, matrix products: 23.5 us -> 35.8 us  [advance(): jnp.einsum('thp,pd->thd', exponent.astype(jnp.bfloat16), key_block[:, hea...]
    dynamic_update_slice x0 -> x7, local copies, waits for them, and re-layouts: none -> 9.06 us  [gather_around(): lax.dynamic_update_slice_in_dim(full, x, (here - far) % ways * step, axis...]
  transfers between devices with their start and end apart: 4 -> 10, of which waited for: 4 -> 10; matrix products, arithmetic and copies ran while one was open for 4% -> 6% of each run, Pallas kernels for 0% -> 0%
where the time goes in v1:
time: 344 us; the launch traced here: 343 us
  waiting for transfers between devices  185 us (54%)
  matrix products  79.4 us (23%)
  local copies, waits for them, and re-layouts  34.7 us (10%)
  other arithmetic  22.4 us (7%)
  between operations  15.4 us (4%)
  loops' own time  5.68 us (2%)
    ppermute x7, waiting for transfers between devices, gather_around(): x = lax.ppermute(x, axis, [(d, (d + 1) % ways) for d in range(ways)])  64.5 us
    reduce_scatter x1, waiting for transfers between devices, shards(): lax.psum_scatter(jnp.dot(hidden, contract_weight, preferred_element_type=...  45.2 us
    all_gather x1, waiting for transfers between devices, folded_attention(): portion = lax.all_gather(selected, 'member', axis=0, tiled=True)  38.2 us
    all_gather x1, waiting for transfers between devices, shards(): every_block = lax.all_gather(prefix_cache, 'group', axis=0, tiled=True)  36.7 us
    dot_general x8, matrix products, advance(): jnp.einsum('thp,pd->thd', exponent.astype(jnp.bfloat16), key_block[:, hea...  35.8 us
    dot_general x8, matrix products, advance(): jnp.einsum('thd,pd->thp', queries, key_block[:, :head_size], preferred_el...  17.7 us
    dot_general x1, matrix products, shards(): jnp.dot(hidden, contract_weight, preferred_element_type=jnp.float32)  15.1 us
    while x24, local copies, waits for them, and re-layouts  14.4 us
  transfers between devices with their start and end apart: 10, of which 10 were waited for; matrix products, arithmetic and copies ran while one was open for 6% of the time, Pallas kernels for 0%

profile of v1, /device:TPU:0, one launch (start us, length us, event | category | flops | bytes accessed | tf_op | source)
XLA Modules:
  0.0 343.3 jit_solution(2960412460318985349)
XLA Ops:
  10.5 36.7 %all-gather.4.cloned.1.call-done = bf16[4,1024,256]{2,1,0:T(8,128)(2,1)} async-done(((bf16[1,1024,256]{2,1,0:T(8,128)(2,1)}), bf16[4,1024,256]{2,1,0:T(8,128)(2,1)}) %all-gather.4.cloned.1.call-update) | async-done | bytes 2097168 | tf_op jit(solution)/shard_map/all_gather | solution.py:120
  51.8 5.0 %fusion.30 = bf16[16,16,8,128]{3,2,1,0:T(8,128)(2,1)S(1)} fusion(bf16[2048,2048]{1,0:T(8,128)(2,1)} %param.23, bf16[1,128,2048]{2,1,0:T(8,128)(2,1)} %param.16, f32[2048]{0:T(1024)} %param.22, f32[2048]{0:T(1024)} %param.21, f32[128]{0:T(128)S(1)} %add_rsqrt_fusion.1, f32[128]{0:T(128)S(1)} %broadcast_multiply_fusion.1), kind=kOutput, calls=%fused_computation.39 | convolution fusion | flops 1075576832 | bytes 9454592 | tf_op jit(solution)/shard_map/dot_general | solution.py:124
  58.2 38.2 %all-gather.6.cloned.1.call-done = bf16[1,8192,256]{2,1,0:T(8,128)(2,1)} async-done(((bf16[1,1024,256]{2,1,0:T(8,128)(2,1)}), bf16[1,8192,256]{2,1,0:T(8,128)(2,1)}) %all-gather.6.cloned.1.call-update) | async-done | bytes 4194320 | tf_op jit(solution)/shard_map/all_gather | solution.py:61
  96.4 89.6 %while.14 = (s32[]{:T(128)}, f32[128,16,128]{2,0,1:T(8,128)S(1)}, f32[128,16]{0,1:T(8,128)S(1)}, f32[128,16]{0,1:T(8,128)S(1)}, s32[8]{0:T(128)S(1)}, /*index=5*...) while((s32[]{:T(128)}, f32[128,16,128]{2,0,1:T(8,128)S(1)}, ...), condition=%wide.region_10.11_spmd, body=%wide.region_7.10_spmd.sunk | while | flops 1091047424 | bytes 61997284 | solution.py:86
  97.7 2.2 bitcast_reduce_fusion.2
  103.1 4.5 %fusion.69 = f32[128,16,128]{2,0,1:T(8,128)S(1)} fusion(f32[1024,128,16]{1,0,2:T(8,128)} %copy-done.1, f32[128,16]{0,1:T(8,128)S(1)} %max.4, f32[128,16,128]{2,0,1:T(8,128)S(1)} %get-tuple-element.154, f32[128,16]{0,1:T(8,128)S(1)} %get-tuple-element.139, bf16[8192,256]{1,0:T(8,128)(2,1)} %get-tuple-element.170, s32[]{:T(128)S(6)} %select_n.116, ...), kind=kOutput, calls=%fused_computation.8.clone.1 | convolution fusion | flops 543686656 | bytes 10764296 | tf_op jit(solution)/shard_map/while/body/eval_jaxpr/thp,pd->thd/dot_general | solution.py:78
  108.9 2.2 bitcast_reduce_fusion.2
  114.3 4.5 %fusion.69 = f32[128,16,128]{2,0,1:T(8,128)S(1)} fusion(f32[1024,128,16]{1,0,2:T(8,128)} %copy-done.1, f32[128,16]{0,1:T(8,128)S(1)} %max.4, f32[128,16,128]{2,0,1:T(8,128)S(1)} %get-tuple-element.154, f32[128,16]{0,1:T(8,128)S(1)} %get-tuple-element.139, bf16[8192,256]{1,0:T(8,128)(2,1)} %get-tuple-element.170, s32[]{:T(128)S(6)} %select_n.116, ...), kind=kOutput, calls=%fused_computation.8.clone.1 | convolution fusion | flops 543686656 | bytes 10764296 | tf_op jit(solution)/shard_map/while/body/eval_jaxpr/thp,pd->thd/dot_general | solution.py:78
  120.1 2.2 bitcast_reduce_fusion.2
  125.5 4.5 %fusion.69 = f32[128,16,128]{2,0,1:T(8,128)S(1)} fusion(f32[1024,128,16]{1,0,2:T(8,128)} %copy-done.1, f32[128,16]{0,1:T(8,128)S(1)} %max.4, f32[128,16,128]{2,0,1:T(8,128)S(1)} %get-tuple-element.154, f32[128,16]{0,1:T(8,128)S(1)} %get-tuple-element.139, bf16[8192,256]{1,0:T(8,128)(2,1)} %get-tuple-element.170, s32[]{:T(128)S(6)} %select_n.116, ...), kind=kOutput, calls=%fused_computation.8.clone.1 | convolution fusion | flops 543686656 | bytes 10764296 | tf_op jit(solution)/shard_map/while/body/eval_jaxpr/thp,pd->thd/dot_general | solution.py:78
  131.3 2.2 bitcast_reduce_fusion.2
  136.7 4.5 %fusion.69 = f32[128,16,128]{2,0,1:T(8,128)S(1)} fusion(f32[1024,128,16]{1,0,2:T(8,128)} %copy-done.1, f32[128,16]{0,1:T(8,128)S(1)} %max.4, f32[128,16,128]{2,0,1:T(8,128)S(1)} %get-tuple-element.154, f32[128,16]{0,1:T(8,128)S(1)} %get-tuple-element.139, bf16[8192,256]{1,0:T(8,128)(2,1)} %get-tuple-element.170, s32[]{:T(128)S(6)} %select_n.116, ...), kind=kOutput, calls=%fused_computation.8.clone.1 | convolution fusion | flops 543686656 | bytes 10764296 | tf_op jit(solution)/shard_map/while/body/eval_jaxpr/thp,pd->thd/dot_general | solution.py:78
  142.5 2.2 bitcast_reduce_fusion.2
  147.9 4.5 %fusion.69 = f32[128,16,128]{2,0,1:T(8,128)S(1)} fusion(f32[1024,128,16]{1,0,2:T(8,128)} %copy-done.1, f32[128,16]{0,1:T(8,128)S(1)} %max.4, f32[128,16,128]{2,0,1:T(8,128)S(1)} %get-tuple-element.154, f32[128,16]{0,1:T(8,128)S(1)} %get-tuple-element.139, bf16[8192,256]{1,0:T(8,128)(2,1)} %get-tuple-element.170, s32[]{:T(128)S(6)} %select_n.116, ...), kind=kOutput, calls=%fused_computation.8.clone.1 | convolution fusion | flops 543686656 | bytes 10764296 | tf_op jit(solution)/shard_map/while/body/eval_jaxpr/thp,pd->thd/dot_general | solution.py:78
  153.7 2.2 bitcast_reduce_fusion.2
  159.1 4.5 %fusion.69 = f32[128,16,128]{2,0,1:T(8,128)S(1)} fusion(f32[1024,128,16]{1,0,2:T(8,128)} %copy-done.1, f32[128,16]{0,1:T(8,128)S(1)} %max.4, f32[128,16,128]{2,0,1:T(8,128)S(1)} %get-tuple-element.154, f32[128,16]{0,1:T(8,128)S(1)} %get-tuple-element.139, bf16[8192,256]{1,0:T(8,128)(2,1)} %get-tuple-element.170, s32[]{:T(128)S(6)} %select_n.116, ...), kind=kOutput, calls=%fused_computation.8.clone.1 | convolution fusion | flops 543686656 | bytes 10764296 | tf_op jit(solution)/shard_map/while/body/eval_jaxpr/thp,pd->thd/dot_general | solution.py:78
  164.9 2.2 bitcast_reduce_fusion.2
  170.3 4.5 %fusion.69 = f32[128,16,128]{2,0,1:T(8,128)S(1)} fusion(f32[1024,128,16]{1,0,2:T(8,128)} %copy-done.1, f32[128,16]{0,1:T(8,128)S(1)} %max.4, f32[128,16,128]{2,0,1:T(8,128)S(1)} %get-tuple-element.154, f32[128,16]{0,1:T(8,128)S(1)} %get-tuple-element.139, bf16[8192,256]{1,0:T(8,128)(2,1)} %get-tuple-element.170, s32[]{:T(128)S(6)} %select_n.116, ...), kind=kOutput, calls=%fused_computation.8.clone.1 | convolution fusion | flops 543686656 | bytes 10764296 | tf_op jit(solution)/shard_map/while/body/eval_jaxpr/thp,pd->thd/dot_general | solution.py:78
  176.1 2.2 bitcast_reduce_fusion.2
  181.5 4.5 %fusion.69 = f32[128,16,128]{2,0,1:T(8,128)S(1)} fusion(f32[1024,128,16]{1,0,2:T(8,128)} %copy-done.1, f32[128,16]{0,1:T(8,128)S(1)} %max.4, f32[128,16,128]{2,0,1:T(8,128)S(1)} %get-tuple-element.154, f32[128,16]{0,1:T(8,128)S(1)} %get-tuple-element.139, bf16[8192,256]{1,0:T(8,128)(2,1)} %get-tuple-element.170, s32[]{:T(128)S(6)} %select_n.116, ...), kind=kOutput, calls=%fused_computation.8.clone.1 | convolution fusion | flops 543686656 | bytes 10764296 | tf_op jit(solution)/shard_map/while/body/eval_jaxpr/thp,pd->thd/dot_general | solution.py:78
  188.7 4.7 %fusion.51 = (f32[128]{0:T(128)S(1)}, f32[128,2048]{1,0:T(8,128)S(1)}) fusion(bf16[128,2048]{0,1:T(8,128)(2,1)S(1)} %bitcast.88, bf16[2048,2048]{1,0:T(8,128)(2,1)} %param.25, bf16[1,128,2048]{2,1,0:T(8,128)(2,1)S(1)} %copy-done.2), kind=kOutput, calls=%fused_computation.84 | convolution fusion | flops 1074528128 | bytes 10486272 | tf_op jit(solution)/shard_map/dot_general | solution.py:130
  193.8 2.5 broadcast_in_dim.56
  197.6 10.1 %collective-permute-done = bf16[128,2048]{1,0:T(8,128)(2,1)S(1)} collective-permute-done((bf16[128,2048]{1,0:T(8,128)(2,1)S(1)}, bf16[128,2048]{1,0:T(8,128)(2,1)S(1)}, u32[]{:S(2)}, u32[]{:S(2)}) %collective-permute-start) | collective-permute-done | bytes 524320 | tf_op jit(solution)/shard_map/ppermute | solution.py:16
  207.7 10.4 %collective-permute-done.1 = bf16[128,2048]{1,0:T(8,128)(2,1)S(1)} collective-permute-done((bf16[128,2048]{1,0:T(8,128)(2,1)S(1)}, bf16[128,2048]{1,0:T(8,128)(2,1)S(1)}, u32[]{:S(2)}, u32[]{:S(2)}) %collective-permute-start.1) | collective-permute-done | bytes 524320 | tf_op jit(solution)/shard_map/ppermute | solution.py:16
  218.1 10.4 %collective-permute-done.2 = bf16[128,2048]{1,0:T(8,128)(2,1)S(1)} collective-permute-done((bf16[128,2048]{1,0:T(8,128)(2,1)S(1)}, bf16[128,2048]{1,0:T(8,128)(2,1)S(1)}, u32[]{:S(2)}, u32[]{:S(2)}) %collective-permute-start.2) | collective-permute-done | bytes 524320 | tf_op jit(solution)/shard_map/ppermute | solution.py:16
  228.5 10.4 %collective-permute-done.3 = bf16[128,2048]{1,0:T(8,128)(2,1)S(1)} collective-permute-done((bf16[128,2048]{1,0:T(8,128)(2,1)S(1)}, bf16[128,2048]{1,0:T(8,128)(2,1)S(1)}, u32[]{:S(2)}, u32[]{:S(2)}) %collective-permute-start.3) | collective-permute-done | bytes 524320 | tf_op jit(solution)/shard_map/ppermute | solution.py:16
  239.1 10.4 %collective-permute-done.4 = bf16[128,2048]{1,0:T(8,128)(2,1)} collective-permute-done((bf16[128,2048]{1,0:T(8,128)(2,1)S(1)}, bf16[128,2048]{1,0:T(8,128)(2,1)}, u32[]{:S(2)}, u32[]{:S(2)}) %collective-permute-start.4) | collective-permute-done | bytes 524320 | tf_op jit(solution)/shard_map/ppermute | solution.py:16
  254.1 6.0 %collective-permute-done.5 = bf16[128,2048]{1,0:T(8,128)(2,1)S(1)} collective-permute-done((bf16[128,2048]{1,0:T(8,128)(2,1)}, bf16[128,2048]{1,0:T(8,128)(2,1)S(1)}, u32[]{:S(2)}, u32[]{:S(2)}) %collective-permute-start.5) | collective-permute-done | bytes 524320 | tf_op jit(solution)/shard_map/ppermute | solution.py:16
  263.7 6.8 %collective-permute-done.6 = bf16[128,2048]{1,0:T(8,128)(2,1)S(1)} collective-permute-done((bf16[128,2048]{1,0:T(8,128)(2,1)S(1)}, bf16[128,2048]{1,0:T(8,128)(2,1)S(1)}, u32[]{:S(2)}, u32[]{:S(2)}) %collective-permute-start.6) | collective-permute-done | bytes 524320 | tf_op jit(solution)/shard_map/ppermute | solution.py:16
  271.3 15.1 %convolution_convert_fusion = bf16[1024,2048]{1,0:T(8,128)(2,1)} fusion(bf16[1024,2048]{1,0:T(8,128)(2,1)} %param.29, bf16[1024,2048]{1,0:T(8,128)(2,1)} %constant_dynamic-update-slice_fusion, bf16[2048,1024]{1,0:T(8,128)(2,1)} %param.28), kind=kOutput, calls=%fused_computation.25 | convolution fusion | flops 8601468928 | bytes 16777216 | tf_op jit(solution)/shard_map/dot_general | solution.py:139
  289.5 45.2 %reduce-scatter.2.cloned.1.call-done = bf16[128,2048]{1,0:T(8,128)(2,1)} async-done(((bf16[1024,2048]{1,0:T(8,128)(2,1)}), bf16[128,2048]{1,0:T(8,128)(2,1)}) %reduce-scatter.2.cloned.1.call-update) | async-done | bytes 524304 | tf_op jit(solution)/shard_map/reduce_scatter | solution.py:138
  334.8 2.0 fusion.39
  (118 shorter events, 54.7 us)
Async XLA Ops:
  6.5 50.4 %copy-start = (bf16[2048,256]{1,0:T(8,128)(2,1)S(1)}, bf16[2048,256]{1,0:T(8,128)(2,1)}, u32[]{:S(2)}) copy-start(bf16[2048,256]{1,0:T(8,128)(2,1)} %param.24) | copy-start | bytes 3145732
  6.5 40.7 %all-gather.4.cloned.1.call-start = ((), (), s32[]{:S(2)}) async-start(), calls=%async_computation.1 | async-start | bytes 2621440 | tf_op jit(solution)/shard_map/all_gather | solution.py:120
  7.3 89.2 %all-gather.6.cloned.1.call-start = ((), (), s32[]{:S(2)}) async-start(), calls=%async_computation.3 | async-start | bytes 4718592 | tf_op jit(solution)/shard_map/all_gather | solution.py:61
  49.1 285.6 %reduce-scatter.2.cloned.1.call-start = ((), (), s32[]{:S(2)}) async-start(), calls=%async_computation.2 | async-start | bytes 4718592 | tf_op jit(solution)/shard_map/reduce_scatter | solution.py:138
  51.7 5.2 %copy-start.2 = (bf16[1,128,2048]{2,1,0:T(8,128)(2,1)S(1)}, bf16[1,128,2048]{2,1,0:T(8,128)(2,1)}, u32[]{:S(2)}) copy-start(bf16[1,128,2048]{2,1,0:T(8,128)(2,1)} %param.16) | copy-start | bytes 1572868
  51.7 5.2 %copy-start.7 = (f32[2048]{0:T(1024)S(1)}, f32[2048]{0:T(1024)}, u32[]{:S(2)}) copy-start(f32[2048]{0:T(1024)} %param.22) | copy-start | bytes 24580
  51.8 5.2 %copy-start.8 = (f32[2048]{0:T(1024)S(1)}, f32[2048]{0:T(1024)}, u32[]{:S(2)}) copy-start(f32[2048]{0:T(1024)} %param.21) | copy-start | bytes 24580
  99.9 3.2 copy-start.1
  111.1 3.2 copy-start.1
  122.3 3.2 copy-start.1
  133.5 3.2 copy-start.1
  144.7 3.2 copy-start.1
  155.9 3.2 copy-start.1
  167.1 3.2 copy-start.1
  178.3 3.2 copy-start.1
  193.5 2.8 copy-start.5
  193.5 2.8 copy-start.6
  197.3 10.4 %collective-permute-start = (bf16[128,2048]{1,0:T(8,128)(2,1)S(1)}, bf16[128,2048]{1,0:T(8,128)(2,1)S(1)}, u32[]{:S(2)}, u32[]{:S(2)}) collective-permute-start(bf16[128,2048]{1,0:T(8,128)(2,1)S(1)} %get-tuple-element.83), channel_id=1, source_target_pairs={{0,1},{1,2},{2,3},{3,4},{4,5},{5,6},{6,7},{7,0},{8,9},{9,10},{10,1... | collective-permute-start | bytes 1572872 | tf_op jit(solution)/shard_map/ppermute | solution.py:16
  207.7 10.4 %collective-permute-start.1 = (bf16[128,2048]{1,0:T(8,128)(2,1)S(1)}, bf16[128,2048]{1,0:T(8,128)(2,1)S(1)}, u32[]{:S(2)}, u32[]{:S(2)}) collective-permute-start(bf16[128,2048]{1,0:T(8,128)(2,1)S(1)} %collective-permute-done), channel_id=1, source_target_pairs={{0,1},{1,2},{2,3},{3,4},{4,5},{5,6},{6,7},{7,0},{8,9},{9,10},{10,1... | collective-permute-start | bytes 1572872 | tf_op jit(solution)/shard_map/ppermute | solution.py:16
  218.1 20.8 %copy-start.3 = (bf16[128,2048]{1,0:T(8,128)(2,1)}, bf16[128,2048]{1,0:T(8,128)(2,1)S(1)}, u32[]{:S(2)}) copy-start(bf16[128,2048]{1,0:T(8,128)(2,1)S(1)} %collective-permute-done.1) | copy-start | bytes 1572868
  218.1 10.4 %collective-permute-start.2 = (bf16[128,2048]{1,0:T(8,128)(2,1)S(1)}, bf16[128,2048]{1,0:T(8,128)(2,1)S(1)}, u32[]{:S(2)}, u32[]{:S(2)}) collective-permute-start(bf16[128,2048]{1,0:T(8,128)(2,1)S(1)} %collective-permute-done.1), channel_id=1, source_target_pairs={{0,1},{1,2},{2,3},{3,4},{4,5},{5,6},{6,7},{7,0},{8,9},{9,10},{10,1... | collective-permute-start | bytes 1572872 | tf_op jit(solution)/shard_map/ppermute | solution.py:16
  228.5 10.4 %copy-start.4 = (bf16[128,2048]{1,0:T(8,128)(2,1)}, bf16[128,2048]{1,0:T(8,128)(2,1)S(1)}, u32[]{:S(2)}) copy-start(bf16[128,2048]{1,0:T(8,128)(2,1)S(1)} %collective-permute-done.2) | copy-start | bytes 1572868
  228.5 10.4 %collective-permute-start.3 = (bf16[128,2048]{1,0:T(8,128)(2,1)S(1)}, bf16[128,2048]{1,0:T(8,128)(2,1)S(1)}, u32[]{:S(2)}, u32[]{:S(2)}) collective-permute-start(bf16[128,2048]{1,0:T(8,128)(2,1)S(1)} %collective-permute-done.2), channel_id=1, source_target_pairs={{0,1},{1,2},{2,3},{3,4},{4,5},{5,6},{6,7},{7,0},{8,9},{9,10},{10,1... | collective-permute-start | bytes 1572872 | tf_op jit(solution)/shard_map/ppermute | solution.py:16
  238.9 10.5 %collective-permute-start.4 = (bf16[128,2048]{1,0:T(8,128)(2,1)S(1)}, bf16[128,2048]{1,0:T(8,128)(2,1)}, u32[]{:S(2)}, u32[]{:S(2)}) collective-permute-start(bf16[128,2048]{1,0:T(8,128)(2,1)S(1)} %collective-permute-done.3), channel_id=1, source_target_pairs={{0,1},{1,2},{2,3},{3,4},{4,5},{5,6},{6,7},{7,0},{8,9},{9,10},{10,1... | collective-permute-start | bytes 1572872 | tf_op jit(solution)/shard_map/ppermute | solution.py:16
  249.5 10.6 %collective-permute-start.5 = (bf16[128,2048]{1,0:T(8,128)(2,1)}, bf16[128,2048]{1,0:T(8,128)(2,1)S(1)}, u32[]{:S(2)}, u32[]{:S(2)}) collective-permute-start(bf16[128,2048]{1,0:T(8,128)(2,1)} %collective-permute-done.4), channel_id=1, source_target_pairs={{0,1},{1,2},{2,3},{3,4},{4,5},{5,6},{6,7},{7,0},{8,9},{9,10},{10,1... | collective-permute-start | bytes 1572872 | tf_op jit(solution)/shard_map/ppermute | solution.py:16
  260.1 10.4 %collective-permute-start.6 = (bf16[128,2048]{1,0:T(8,128)(2,1)S(1)}, bf16[128,2048]{1,0:T(8,128)(2,1)S(1)}, u32[]{:S(2)}, u32[]{:S(2)}) collective-permute-start(bf16[128,2048]{1,0:T(8,128)(2,1)S(1)} %collective-permute-done.5), channel_id=1, source_target_pairs={{0,1},{1,2},{2,3},{3,4},{4,5},{5,6},{6,7},{7,0},{8,9},{9,10},{10,1... | collective-permute-start | bytes 1572872 | tf_op jit(solution)/shard_map/ppermute | solution.py:16
  286.5 0.7 copy-start.9
  286.5 1.3 copy-start.10
Sparse Core Ops, SparseCore 0:
  9.2 38.0 all-gather.3
  49.3 47.1 all-gather.5
  286.6 48.1 reduce-scatter.1
